TPU v7x, 32 devices: a whole 2x2x4 slice. The times are simulated.
32 devices in a mesh: slab: 4 (over x, core), grp: 8 (over z, y).
Axes of the slice: x: 2, y: 2, z: 4, core: 2. Of those that a mesh axis runs over, the one named last changes fastest.
Arguments:
- raw_frames: bfloat16 [256, 48, 10752], P('grp', 'slab'), may hold values from -700 to 700
- mask_index: int32 [57344], P(('slab', 'grp')), may hold values from 0 to 516095, as said below
- subspace: bfloat16 [1200, 57344], P(None, ('slab', 'grp')), may hold values from -6 to 6
- rotation: bfloat16 [1456, 1200], replicated, may hold values from -0.15625 to 0.15625
Outputs:
- gram: float32 [1456, 1456], P('grp')
- new_subspace: bfloat16 [1200, 57344], P(None, ('slab', 'grp'))
Inputs may be any that keep to these rules, and one draw needn't show every extreme that they name: `mask_index`: entries are distinct flat grid positions that come in runs of 128 consecutive positions, each run starting at a multiple of 128; the 14336 entries of aligned block s lie in z planes s * 12 to (s + 1) * 12 - 1 and rise within the block; the first 3584 of a block lie in its lowest 3 planes, the last 3584 in its highest 3 planes, the others in the planes between.
All inputs are finite; a program needn't handle non-finite values.
Results may differ from a plain program's by a relative error of at most 0.006.
Values may be sent and summed in bfloat16 or wider, within the bound.
A program may use at most 192 MiB of HBM per device.

v0:
```python
import math
import jax
import jax.numpy as jnp
from jax import lax
from jax.sharding import PartitionSpec as P

NX = 96
RUN = 128
RAD = 3
K = 1200
smooth_sigma = 1.0617
epsilon = 1e-06


def padded_2(cells, sides, width):
    for axis, dim in sides:
        count = lax.axis_size(axis)
        ends = count - 1
        head = lax.slice_in_dim(cells, 0, width, axis=dim)
        tail = lax.slice_in_dim(cells, cells.shape[dim] - width, cells.shape[dim], axis=dim)
        cells = jnp.concatenate(
            [
                lax.ppermute(tail, axis, [(i, (i + 1) % count) for i in range(ends)]),
                cells,
                lax.ppermute(head, axis, [((i + 1) % count, i) for i in range(ends)]),
            ],
            axis=dim,
        )
    return cells


def tap_weights():
    unscaled = [
        math.exp(-offset * offset / (2.0 * smooth_sigma * smooth_sigma))
        for offset in range(-RAD, RAD + 1)
    ]
    summed = sum(unscaled)
    return [weight / summed for weight in unscaled]


def along_rows(volume):
    weights = tap_weights()
    extent = volume.shape[-1]
    column = lax.broadcasted_iota(jnp.int32, (extent,), 0) % NX
    padded = jnp.pad(volume, [(0, 0)] * (volume.ndim - 1) + [(RAD, RAD)])
    summed = jnp.zeros(volume.shape, jnp.float32)
    for offset in range(-RAD, RAD + 1):
        shifted = lax.slice_in_dim(
            padded, RAD + offset, RAD + offset + extent, axis=volume.ndim - 1
        )
        inside = (column + offset >= 0) & (column + offset < NX)
        summed = summed + weights[offset + RAD] * jnp.where(inside, shifted, 0.0)
    return summed


def along_columns(volume):
    weights = tap_weights()
    extent = volume.shape[-1]
    reach_cells = RAD * NX
    padded = jnp.pad(volume, [(0, 0)] * (volume.ndim - 1) + [(reach_cells, reach_cells)])
    summed = jnp.zeros(volume.shape, jnp.float32)
    for offset in range(-RAD, RAD + 1):
        begin = reach_cells + offset * NX
        shifted = lax.slice_in_dim(padded, begin, begin + extent, axis=volume.ndim - 1)
        summed = summed + weights[offset + RAD] * shifted
    return summed


def along_depth(padded, slab_depth):
    weights = tap_weights()
    summed = None
    for offset in range(-RAD, RAD + 1):
        shifted = lax.slice_in_dim(
            padded, RAD + offset, RAD + offset + slab_depth, axis=padded.ndim - 2
        )
        term = weights[offset + RAD] * shifted
        summed = term if summed is None else summed + term
    return summed


def pick_columns(matrix, wanted):
    row_total = matrix.shape[0]
    blocked = matrix.reshape(row_total, matrix.shape[1] // RUN, RUN)
    run_starts = wanted.reshape(-1, RUN)[:, 0] // RUN
    picked_runs = jnp.take(blocked, run_starts, axis=1)
    return picked_runs.reshape(row_total, wanted.shape[0])


def body(raw_frames, mask_index, subspace, rotation):
    frames_here = raw_frames.shape[0]
    slab_depth = raw_frames.shape[1]
    extent = raw_frames.shape[2]
    per_device = subspace.shape[1]
    group_count = lax.axis_size("grp")
    masked = per_device * lax.axis_size("slab") * group_count
    positions = lax.all_gather(mask_index, "grp", axis=0, tiled=True) - lax.axis_index("slab") * (
        slab_depth * extent
    )
    padded = padded_2(raw_frames, (("slab", 1),), RAD)
    planar = along_columns(along_rows(padded.astype(jnp.float32)))
    smoothed = (
        along_depth(planar, slab_depth)
        .reshape(frames_here, slab_depth * extent)
        .astype(jnp.bfloat16)
    )
    picked = pick_columns(smoothed, positions)
    regrouped = lax.all_to_all(picked, "grp", split_axis=1, concat_axis=0, tiled=True)
    frame_count = regrouped.shape[0]
    subject_frames = frame_count // 2
    halves = regrouped.astype(jnp.float32).reshape(2, subject_frames, per_device)
    centered = (halves - jnp.mean(halves, axis=1, keepdims=True)).astype(jnp.bfloat16)
    order_rows = K + frame_count
    stacked = jnp.concatenate([subspace, centered.reshape(frame_count, per_device)], 0)
    widened = centered.astype(jnp.float32)
    power = lax.psum(jnp.sum(widened * widened, axis=(1, 2)), ("slab", "grp"))
    rows_here = order_rows // group_count
    first_row = lax.axis_index("grp") * rows_here
    gram_raw = lax.psum(
        jnp.dot(stacked, stacked.T, preferred_element_type=jnp.float32), ("slab", "grp")
    )
    owned = lax.dynamic_slice_in_dim(gram_raw, first_row, rows_here, 0)
    scales = lax.rsqrt(power / (masked * subject_frames) + epsilon)
    row_scale = jnp.concatenate([jnp.ones((K,), jnp.float32), jnp.repeat(scales, subject_frames)])
    owned_scale = lax.dynamic_slice_in_dim(row_scale, first_row, rows_here, 0)
    gram_rows = owned * (owned_scale[:, None] * row_scale[None, :]) / masked
    contract = (((0,), (0,)), ((), ()))
    from_basis = lax.dot_general(
        rotation[:K], subspace, contract, preferred_element_type=jnp.float32
    )
    from_first = lax.dot_general(
        rotation[K : K + subject_frames], centered[0], contract, preferred_element_type=jnp.float32
    )
    from_second = lax.dot_general(
        rotation[K + subject_frames :], centered[1], contract, preferred_element_type=jnp.float32
    )
    new_subspace = (from_basis + scales[0] * from_first + scales[1] * from_second).astype(
        jnp.bfloat16
    )
    return (gram_rows, new_subspace)


def solution(mesh):
    placed = (P("grp", "slab", None), P(("slab", "grp")), P(None, ("slab", "grp")), P())
    return jax.shard_map(
        body,
        mesh=mesh,
        in_specs=placed,
        out_specs=(P("grp", None), P(None, ("slab", "grp"))),
        check_vma=False,
    )
```

profile of v0, /device:TPU:0, one launch (start us, length us, event | category | flops | bytes accessed | tf_op | source)
XLA Modules:
  0.0 511.2 jit_solution(89150723595462847)
XLA Ops:
  7.2 4.5 fusion.61
  11.7 2.5 collective-permute-start
  14.2 1.3 collective-permute-start.1
  15.5 0.7 reshape.63
  16.2 31.9 %all-gather = s32[8,1,1792]{2,1,0:T(1,128)S(1)} all-gather(s32[1,1,1792]{2,1,0:T(1,128)S(1)} %reshape.63), channel_id=1, replica_groups=mesh['slab'=4,'grp'=8] {'grp'}, dimensions={0}, use_global_device_ids=true | all-gather | bytes 64512 | tf_op jit(solution)/shard_map/all_gather | solution.py:96
  48.9 12.9 %maximum_convert_fusion = f32[32,18,10752]{2,0,1:T(8,128)} fusion(bf16[32,3,10752]{2,0,1:T(8,128)(2,1)} %collective-permute-done.1, bf16[32,12,10752]{2,0,1:T(8,128)(2,1)} %param.4, bf16[32,3,10752]{2,0,1:T(8,128)(2,1)S(1)} %collective-permute-done), kind=kLoop, calls=%fused_computation.29 | loop fusion | flops 18579456 | bytes 37158912 | tf_op jit(solution)/shard_map/convert_element_type | solution.py:100
  61.8 64.2 %multiply_add_fusion.1 = f32[32,18,10752]{2,0,1:T(8,128)} fusion(f32[32,18,10752]{2,0,1:T(8,128)} %maximum_convert_fusion, pred[10752]{0:T(1024)(128)(4,1)S(1)} %get-tuple-element.8, pred[10752]{0:T(1024)(128)(4,1)S(1)} %get-tuple-element.9, pred[10752]{0:T(1024)(128)(4,1)S(1)} %get-tuple-element.10, pred[10752]{0:T(1024)(128)(4,1)S(1)} %fusion.58, ...), kind=kLoop, calls=%fused_computation.7 | loop fusion | flops 123863040 | bytes 49620480 | tf_op jit(solution)/shard_map/add | solution.py:52
  125.9 64.0 %multiply_add_fusion = f32[32,18,10752]{2,0,1:T(8,128)} fusion(f32[32,18,10752]{2,0,1:T(8,128)} %multiply_add_fusion.1), kind=kLoop, calls=%fused_computation.1 | loop fusion | flops 80510976 | bytes 49545216 | tf_op jit(solution)/shard_map/add | solution.py:65
  189.9 40.4 %fusion.9 = bf16[32,12,10752]{2,0,1:T(8,128)(2,1)} fusion(f32[32,18,10752]{2,0,1:T(8,128)} %multiply_add_fusion), kind=kLoop, calls=%fused_computation.17 | loop fusion | flops 57802752 | bytes 123863040 | tf_op jit(solution)/shard_map/convert_element_type | solution.py:104
  230.3 12.2 %copy.23 = bf16[32,12,10752]{2,1,0:T(8,128)(2,1)} copy(bf16[32,12,10752]{2,0,1:T(8,128)(2,1)} %fusion.9) | data formatting | bytes 16515072 | tf_op jit(solution)/shard_map/convert_element_type | solution.py:104
  242.5 18.6 %convert_element_type.54 = bf16[32,1008,128]{2,1,0:T(8,128)(2,1)} reshape(bf16[32,12,10752]{2,1,0:T(8,128)(2,1)} %copy.23) | data formatting | bytes 16515072 | tf_op jit(solution)/shard_map/convert_element_type | solution.py:104
  261.0 8.6 %copy.24 = bf16[32,1008,128]{2,0,1:T(8,128)(2,1)} copy(bf16[32,1008,128]{2,1,0:T(8,128)(2,1)} %convert_element_type.54) | data formatting | bytes 16515072 | tf_op jit(solution)/shard_map/convert_element_type | solution.py:104
  269.7 4.1 gather_fusion
  274.1 1.0 gather.7
  275.4 24.6 %all_to_all.10 = bf16[32,8,1792]{2,0,1:T(8,128)(2,1)S(1)} all-to-all(bf16[32,8,1792]{2,0,1:T(8,128)(2,1)S(1)} %copy.26), channel_id=1, replica_groups=mesh['slab'=4,'grp'=8] {'grp'}, dimensions={1} | all-to-all | bytes 1835008 | tf_op jit(solution)/shard_map/all_to_all | solution.py:107
  300.5 14.3 %fusion.19 = f32[1456,1456]{1,0:T(8,128)} fusion(bf16[256,1792]{1,0:T(8,128)(2,1)S(1)} %fusion.24, bf16[1200,1792]{1,0:T(8,128)(2,1)} %param.6), kind=kOutput, calls=%fused_computation.37 | convolution fusion | flops 7608287232 | bytes 13698048 | tf_op jit(solution)/shard_map/dot_general | solution.py:119
  314.9 0.4 multiply_reduce_fusion
  315.5 40.8 %psum.15 = f32[2]{0:T(128)S(1)} all-reduce(f32[2]{0:T(128)S(1)} %reduce_sum.37), channel_id=1, replica_groups=mesh['slab'=4,'grp'=8] {'slab','grp'}, use_global_device_ids=true, to_apply=%region_5.6 | all-reduce | flops 2 | bytes 16 | tf_op jit(solution)/shard_map/psum | solution.py:115
  356.7 0.6 fusion.62
  357.4 3.5 fusion.16
  360.9 3.1 fusion.17
  364.0 9.7 %fusion.18 = bf16[1200,1792]{1,0:T(8,128)(2,1)} fusion(f32[1200,1792]{1,0:T(8,128)S(1)} %fusion.17, f32[1200,1792]{1,0:T(8,128)S(1)} %fusion.16, bf16[1200,1792]{1,0:T(8,128)(2,1)} %param.6, bf16[1456,1200]{0,1:T(8,128)(2,1)S(1)} %copy-done), kind=kOutput, calls=%fused_computation.36 | convolution fusion | flops 5167411200 | bytes 28876800 | tf_op jit(solution)/shard_map/dot_general | solution.py:127
  373.7 128.2 %all-reduce.5.cloned.1.call-done = f32[1456,1456]{1,0:T(8,128)} async-done(((f32[1456,1456]{1,0:T(8,128)}), f32[1456,1456]{1,0:T(8,128)}) %all-reduce.5.cloned.1.call-update) | async-done | bytes 8479760 | tf_op jit(solution)/shard_map/psum | solution.py:118
  501.9 2.5 multiply_multiply_fusion
  (35 shorter events, 2.5 us)
Async XLA Ops:
  7.2 494.8 %all-reduce.5.cloned.1.call-start = ((), (), s32[]{:S(2)}) async-start(), calls=%async_computation.1 | async-start | bytes 17891328 | tf_op jit(solution)/shard_map/psum | solution.py:118
  11.7 37.2 %collective-permute-start = (bf16[32,3,10752]{2,0,1:T(8,128)(2,1)}, bf16[32,3,10752]{2,0,1:T(8,128)(2,1)S(1)}, u32[]{:S(2)}, u32[]{:S(2)}) collective-permute-start(bf16[32,3,10752]{2,0,1:T(8,128)(2,1)} %get-tuple-element.4), channel_id=1, source_target_pairs={{0,8},{8,16},{16,24},{1,9},{9,17},{17,25},{2,10},{10,18},{18,26},{... | collective-permute-start | bytes 6193160 | tf_op jit(solution)/shard_map/ppermute | solution.py:23
  14.2 34.6 %collective-permute-start.1 = (bf16[32,3,10752]{2,0,1:T(8,128)(2,1)}, bf16[32,3,10752]{2,0,1:T(8,128)(2,1)}, u32[]{:S(2)}, u32[]{:S(2)}) collective-permute-start(bf16[32,3,10752]{2,0,1:T(8,128)(2,1)} %get-tuple-element.5), channel_id=1, source_target_pairs={{8,0},{16,8},{24,16},{9,1},{17,9},{25,17},{10,2},{18,10},{26,18},{... | collective-permute-start | bytes 6193160 | tf_op jit(solution)/shard_map/ppermute | solution.py:25
  357.4 6.6 %copy-start = (bf16[1456,1200]{0,1:T(8,128)(2,1)S(1)}, bf16[1456,1200]{0,1:T(8,128)(2,1)}, u32[]{:S(2)}) copy-start(bf16[1456,1200]{0,1:T(8,128)(2,1)} %param.7) | copy-start | bytes 10483204
Sparse Core Ops, SparseCore 0:
  315.0 186.8 all-reduce.4
where the time goes:
time: 512 us; the launch traced here: 511 us
  other arithmetic  186 us (36%)
  waiting for transfers between devices  128 us (25%)
  blocking collectives  97.3 us (19%)
  local copies, waits for them, and re-layouts  51.4 us (10%)
  matrix products  30.6 us (6%)
  between operations  14.2 us (3%)
    psum x1, waiting for transfers between devices, body(): lax.psum(jnp.dot(stacked, stacked.T, preferred_element_type=jnp.float32),...  128 us
    add x1, other arithmetic, along_rows(): summed = summed + weights[offset + RAD] * jnp.where(inside, shifted, 0.0)  64.2 us
    add x1, other arithmetic, along_columns(): summed = summed + weights[offset + RAD] * shifted  64 us
    psum x1, blocking collectives, body(): power = lax.psum(jnp.sum(widened * widened, axis=(1, 2)), ('slab', 'grp'))  40.8 us
    convert_element_type x1, other arithmetic, body(): smoothed = along_depth(planar, slab_depth).reshape(frames_here, slab_dept...  40.4 us
    convert_element_type x3, local copies, waits for them, and re-layouts, body(): smoothed = along_depth(planar, slab_depth).reshape(frames_here, slab_dept...  39.4 us
    all_gather x1, blocking collectives, body(): lax.all_gather(mask_index, 'grp', axis=0, tiled=True)  31.9 us
    all_to_all x1, blocking collectives, body(): lax.all_to_all(picked, 'grp', split_axis=1, concat_axis=0, tiled=True)  24.6 us
  transfers between devices with their start and end apart: 3, of which 1 were waited for; matrix products, arithmetic and copies ran while one was open for 4% of the time, Pallas kernels for 0%

commit v1 on v0

--- a/solution.py
+++ b/solution.py
@@ -116,7 +116,7 @@
     rows_here = order_rows // group_count
     first_row = lax.axis_index("grp") * rows_here
     gram_raw = lax.psum(
-        jnp.dot(stacked, stacked.T, preferred_element_type=jnp.float32), ("slab", "grp")
+        lax.psum(jnp.dot(stacked, stacked.T, preferred_element_type=jnp.float32), "grp"), "slab"
     )
     owned = lax.dynamic_slice_in_dim(gram_raw, first_row, rows_here, 0)
     scales = lax.rsqrt(power / (masked * subject_frames) + epsilon)

time: 512 us -> 774 us (1.51)
  waiting for transfers between devices: 128 us -> 390 us
    psum x1, waiting for transfers between devices: 128 us -> 284 us  [body(): lax.psum(jnp.dot(stacked, stacked.T, preferred_element_type=jnp.float32),...]
    psum x0 -> x1, waiting for transfers between devices: none -> 106 us  [body(): lax.psum(lax.psum(jnp.dot(stacked, stacked.T, preferred_element_type=jnp....]
  transfers between devices with their start and end apart: 3 -> 4, of which waited for: 1 -> 2; matrix products, arithmetic and copies ran while one was open for 4% -> 2% of each run, Pallas kernels for 0% -> 0%
where the time goes in v1:
time: 774 us; the launch traced here: 773 us
  waiting for transfers between devices  390 us (50%)
  other arithmetic  186 us (24%)
  blocking collectives  97.1 us (13%)
  local copies, waits for them, and re-layouts  51.4 us (7%)
  matrix products  30.4 us (4%)
  between operations  14.3 us (2%)
    psum x1, waiting for transfers between devices, body(): lax.psum(jnp.dot(stacked, stacked.T, preferred_element_type=jnp.float32),...  284 us
    psum x1, waiting for transfers between devices, body(): lax.psum(lax.psum(jnp.dot(stacked, stacked.T, preferred_element_type=jnp....  106 us
    add x1, other arithmetic, along_rows(): summed = summed + weights[offset + RAD] * jnp.where(inside, shifted, 0.0)  64.2 us
    add x1, other arithmetic, along_columns(): summed = summed + weights[offset + RAD] * shifted  64 us
    psum x1, blocking collectives, body(): power = lax.psum(jnp.sum(widened * widened, axis=(1, 2)), ('slab', 'grp'))  40.6 us
    convert_element_type x1, other arithmetic, body(): smoothed = along_depth(planar, slab_depth).reshape(frames_here, slab_dept...  40.4 us
    convert_element_type x3, local copies, waits for them, and re-layouts, body(): smoothed = along_depth(planar, slab_depth).reshape(frames_here, slab_dept...  39.4 us
    all_gather x1, blocking collectives, body(): lax.all_gather(mask_index, 'grp', axis=0, tiled=True)  31.9 us
  transfers between devices with their start and end apart: 4, of which 2 were waited for; matrix products, arithmetic and copies ran while one was open for 2% of the time, Pallas kernels for 0%

profile of v1, /device:TPU:0, one launch (start us, length us, event | category | flops | bytes accessed | tf_op | source)
XLA Modules:
  0.0 772.7 jit_solution(17878890378840630101)
XLA Ops:
  7.2 4.5 fusion.61
  11.7 2.5 collective-permute-start
  14.2 1.3 collective-permute-start.1
  15.5 0.7 reshape.63
  16.2 31.9 %all-gather = s32[8,1,1792]{2,1,0:T(1,128)S(1)} all-gather(s32[1,1,1792]{2,1,0:T(1,128)S(1)} %reshape.63), channel_id=1, replica_groups=mesh['slab'=4,'grp'=8] {'grp'}, dimensions={0}, use_global_device_ids=true | all-gather | bytes 64512 | tf_op jit(solution)/shard_map/all_gather | solution.py:96
  48.9 12.9 %maximum_convert_fusion = f32[32,18,10752]{2,0,1:T(8,128)} fusion(bf16[32,3,10752]{2,0,1:T(8,128)(2,1)} %collective-permute-done.1, bf16[32,12,10752]{2,0,1:T(8,128)(2,1)} %param.4, bf16[32,3,10752]{2,0,1:T(8,128)(2,1)S(1)} %collective-permute-done), kind=kLoop, calls=%fused_computation.29 | loop fusion | flops 18579456 | bytes 37158912 | tf_op jit(solution)/shard_map/convert_element_type | solution.py:100
  61.8 64.2 %multiply_add_fusion.1 = f32[32,18,10752]{2,0,1:T(8,128)} fusion(f32[32,18,10752]{2,0,1:T(8,128)} %maximum_convert_fusion, pred[10752]{0:T(1024)(128)(4,1)S(1)} %get-tuple-element.8, pred[10752]{0:T(1024)(128)(4,1)S(1)} %get-tuple-element.9, pred[10752]{0:T(1024)(128)(4,1)S(1)} %get-tuple-element.10, pred[10752]{0:T(1024)(128)(4,1)S(1)} %fusion.58, ...), kind=kLoop, calls=%fused_computation.7 | loop fusion | flops 123863040 | bytes 49620480 | tf_op jit(solution)/shard_map/add | solution.py:52
  125.9 64.0 %multiply_add_fusion = f32[32,18,10752]{2,0,1:T(8,128)} fusion(f32[32,18,10752]{2,0,1:T(8,128)} %multiply_add_fusion.1), kind=kLoop, calls=%fused_computation.1 | loop fusion | flops 80510976 | bytes 49545216 | tf_op jit(solution)/shard_map/add | solution.py:65
  189.9 40.4 %fusion.9 = bf16[32,12,10752]{2,0,1:T(8,128)(2,1)} fusion(f32[32,18,10752]{2,0,1:T(8,128)} %multiply_add_fusion), kind=kLoop, calls=%fused_computation.17 | loop fusion | flops 57802752 | bytes 123863040 | tf_op jit(solution)/shard_map/convert_element_type | solution.py:104
  230.3 12.2 %copy.23 = bf16[32,12,10752]{2,1,0:T(8,128)(2,1)} copy(bf16[32,12,10752]{2,0,1:T(8,128)(2,1)} %fusion.9) | data formatting | bytes 16515072 | tf_op jit(solution)/shard_map/convert_element_type | solution.py:104
  242.5 18.6 %convert_element_type.54 = bf16[32,1008,128]{2,1,0:T(8,128)(2,1)} reshape(bf16[32,12,10752]{2,1,0:T(8,128)(2,1)} %copy.23) | data formatting | bytes 16515072 | tf_op jit(solution)/shard_map/convert_element_type | solution.py:104
  261.0 8.6 %copy.24 = bf16[32,1008,128]{2,0,1:T(8,128)(2,1)} copy(bf16[32,1008,128]{2,1,0:T(8,128)(2,1)} %convert_element_type.54) | data formatting | bytes 16515072 | tf_op jit(solution)/shard_map/convert_element_type | solution.py:104
  269.7 4.1 gather_fusion
  274.1 1.0 gather.7
  275.4 24.6 %all_to_all.10 = bf16[32,8,1792]{2,0,1:T(8,128)(2,1)S(1)} all-to-all(bf16[32,8,1792]{2,0,1:T(8,128)(2,1)S(1)} %copy.26), channel_id=1, replica_groups=mesh['slab'=4,'grp'=8] {'grp'}, dimensions={1} | all-to-all | bytes 1835008 | tf_op jit(solution)/shard_map/all_to_all | solution.py:107
  300.5 14.3 %fusion.19 = f32[1456,1456]{1,0:T(8,128)} fusion(bf16[256,1792]{1,0:T(8,128)(2,1)S(1)} %fusion.24, bf16[1200,1792]{1,0:T(8,128)(2,1)} %param.6), kind=kOutput, calls=%fused_computation.37 | convolution fusion | flops 7608287232 | bytes 13698048 | tf_op jit(solution)/shard_map/dot_general | solution.py:119
  314.9 283.8 %all-reduce.6.cloned.1.call-done = f32[1456,1456]{1,0:T(8,128)} async-done(((f32[1456,1456]{1,0:T(8,128)}), f32[1456,1456]{1,0:T(8,128)}) %all-reduce.6.cloned.1.call-update) | async-done | bytes 8479760 | tf_op jit(solution)/shard_map/psum | solution.py:119
  599.3 40.6 %psum.23 = f32[2]{0:T(128)S(1)} all-reduce(f32[2]{0:T(128)S(1)} %reduce_sum.37), channel_id=1, replica_groups=mesh['slab'=4,'grp'=8] {'slab','grp'}, use_global_device_ids=true, to_apply=%region_6.7 | all-reduce | flops 2 | bytes 16 | tf_op jit(solution)/shard_map/psum | solution.py:115
  640.3 0.6 fusion.62
  641.0 3.4 fusion.16
  644.4 3.1 fusion.17
  647.5 9.7 %fusion.18 = bf16[1200,1792]{1,0:T(8,128)(2,1)} fusion(f32[1200,1792]{1,0:T(8,128)S(1)} %fusion.17, f32[1200,1792]{1,0:T(8,128)S(1)} %fusion.16, bf16[1200,1792]{1,0:T(8,128)(2,1)} %param.6, bf16[1456,1200]{0,1:T(8,128)(2,1)S(1)} %copy-done), kind=kOutput, calls=%fused_computation.36 | convolution fusion | flops 5167411200 | bytes 28876800 | tf_op jit(solution)/shard_map/dot_general | solution.py:127
  657.1 106.2 %all-reduce.8.cloned.1.call-done = f32[1456,1456]{1,0:T(8,128)} async-done(((f32[1456,1456]{1,0:T(8,128)}), f32[1456,1456]{1,0:T(8,128)}) %all-reduce.8.cloned.1.call-update) | async-done | bytes 8479760 | tf_op jit(solution)/shard_map/psum | solution.py:118
  763.3 2.5 multiply_multiply_fusion
  (38 shorter events, 3.0 us)
Async XLA Ops:
  7.2 591.5 %all-reduce.6.cloned.1.call-start = ((), (), s32[]{:S(2)}) async-start(), calls=%async_computation.1 | async-start | bytes 17891328 | tf_op jit(solution)/shard_map/psum | solution.py:119
  11.7 37.2 %collective-permute-start = (bf16[32,3,10752]{2,0,1:T(8,128)(2,1)}, bf16[32,3,10752]{2,0,1:T(8,128)(2,1)S(1)}, u32[]{:S(2)}, u32[]{:S(2)}) collective-permute-start(bf16[32,3,10752]{2,0,1:T(8,128)(2,1)} %get-tuple-element.4), channel_id=1, source_target_pairs={{0,8},{8,16},{16,24},{1,9},{9,17},{17,25},{2,10},{10,18},{18,26},{... | collective-permute-start | bytes 6193160 | tf_op jit(solution)/shard_map/ppermute | solution.py:23
  14.2 34.6 %collective-permute-start.1 = (bf16[32,3,10752]{2,0,1:T(8,128)(2,1)}, bf16[32,3,10752]{2,0,1:T(8,128)(2,1)}, u32[]{:S(2)}, u32[]{:S(2)}) collective-permute-start(bf16[32,3,10752]{2,0,1:T(8,128)(2,1)} %get-tuple-element.5), channel_id=1, source_target_pairs={{8,0},{16,8},{24,16},{9,1},{17,9},{25,17},{10,2},{18,10},{26,18},{... | collective-permute-start | bytes 6193160 | tf_op jit(solution)/shard_map/ppermute | solution.py:25
  314.9 448.5 %all-reduce.8.cloned.1.call-start = ((), (), s32[]{:S(2)}) async-start(), calls=%async_computation.2 | async-start | bytes 17891328 | tf_op jit(solution)/shard_map/psum | solution.py:118
  641.0 6.5 copy-start
Sparse Core Ops, SparseCore 0:
  315.0 283.6 all-reduce.5
  601.1 162.1 all-reduce.7
